TPU v7x, 32 devices: a whole 2x2x4 slice. The times are simulated.
32 devices in a mesh: dp: 8 (over y, x, core), tensor: 4 (over z).
Axes of the slice: x: 2, y: 2, z: 4, core: 2. Of those that a mesh axis runs over, the one named last changes fastest.
Arguments:
- latents: bfloat16 [16384, 1280], P('dp'), may hold values from -6 to 6
- norm1_gain: float32 [1280], replicated, may hold values from 0.5 to 1.5
- norm1_shift: float32 [1280], replicated, may hold values from -1.75 to 1.75
- query_weight: bfloat16 [1280, 1280], P(None, 'tensor'), may hold values from -0.15625 to 0.15625
- query_bias: float32 [1280], P('tensor'), may hold values from -1.75 to 1.75
- key_weight: bfloat16 [1280, 1280], P(None, 'tensor'), may hold values from -0.15625 to 0.15625
- value_weight: bfloat16 [1280, 1280], P(None, 'tensor'), may hold values from -0.15625 to 0.15625
- value_bias: float32 [1280], P('tensor'), may hold values from -1.75 to 1.75
- out_weight: bfloat16 [1280, 1280], P('tensor'), may hold values from -0.625 to 0.625
- out_bias: float32 [1280], replicated, may hold values from -1.75 to 1.75
- norm2_gain: float32 [1280], replicated, may hold values from 0.5 to 1.5
- norm2_shift: float32 [1280], replicated, may hold values from -1.75 to 1.75
- hidden_weight: bfloat16 [1280, 1280], P(None, 'tensor'), may hold values from -0.15625 to 0.15625
- hidden_bias: float32 [1280], P('tensor'), may hold values from -1.75 to 1.75
- proj_weight: bfloat16 [1280, 1280], P('tensor'), may hold values from -0.25 to 0.25
- proj_bias: float32 [1280], replicated, may hold values from -1.75 to 1.75
- segments: int32 [16, 1024], P('dp'), may hold values from 0 to 7, never falling along the last dimension, each value on 1 to 512 neighbouring positions
- valid_mask: int32 [16, 1024], P('dp'), may hold values 0 or 1
- cotangent: bfloat16 [16384, 1280], P('dp'), may hold values from -6 to 6
Outputs:
- output: bfloat16 [16384, 1280], P('dp')
- grad_input: float32 [16384, 1280], P('dp')
- grad_norm1_gain: float32 [1280], replicated
- grad_norm1_shift: float32 [1280], replicated
- grad_query_weight: float32 [1280, 1280], P(None, 'tensor')
- grad_query_bias: float32 [1280], P('tensor')
- grad_key_weight: float32 [1280, 1280], P(None, 'tensor')
- grad_value_weight: float32 [1280, 1280], P(None, 'tensor')
- grad_value_bias: float32 [1280], P('tensor')
- grad_out_weight: float32 [1280, 1280], P('tensor')
- grad_out_bias: float32 [1280], replicated
- grad_norm2_gain: float32 [1280], replicated
- grad_norm2_shift: float32 [1280], replicated
- grad_hidden_weight: float32 [1280, 1280], P(None, 'tensor')
- grad_hidden_bias: float32 [1280], P('tensor')
- grad_proj_weight: float32 [1280, 1280], P('tensor')
- grad_proj_bias: float32 [1280], replicated
- rms: float32 [16, 3], P('dp')
Inputs may be any that keep to these rules, and one draw needn't show every extreme that they name: `segments`: in each row segment numbers never fall, each document has 1 to 512 positions, and one has exactly that many.
All inputs are finite; a program needn't handle non-finite values. No bound on the sum of `valid_mask` on one device may be relied on, other than what follows from the above.
Results may differ from a plain program's by a relative error of at most 0.013.
Values sent between devices are 32-bit elements; how exact they have to be, the bound alone decides.
A program may use at most 192 MiB of HBM per device.

v0:
```python
import functools
import math

import jax
import jax.numpy as jnp
from jax import lax
from jax.experimental import pallas as pl
from jax.experimental.pallas import tpu as pltpu
from jax.sharding import PartitionSpec as P

HEAD_DIM = 160
MAX_DOC = 512
EPS = 1e-05
NEG = -1e30
BLK = 256
WIN = 256
LANES = 128
SCALE = 1.0 / math.sqrt(HEAD_DIM)
LOG2E = 1.0 / math.log(2.0)
BF = jnp.bfloat16
F32 = jnp.float32
VMEM_MAX = 60 << 20


def nn(a, b):
    return lax.dot_general(a, b, (((1,), (0,)), ((), ())), preferred_element_type=F32)


def nt(a, b):
    return lax.dot_general(a, b, (((1,), (1,)), ((), ())), preferred_element_type=F32)


def tn(a, b):
    return lax.dot_general(a, b, (((0,), (0,)), ((), ())), preferred_element_type=F32)


def whole(shape):
    return pl.BlockSpec(shape, lambda *_: (0,) * len(shape), pipeline_mode=pl.Buffered(1))


def held(shape):
    return pl.BlockSpec(shape, lambda *_: (0,) * len(shape))


def rows(width):
    return pl.BlockSpec((BLK, width), lambda i: (i, 0))


def column_of(row):
    n = row.shape[1]
    eye = lax.broadcasted_iota(jnp.int32, (n, n), 0) == lax.broadcasted_iota(jnp.int32, (n, n), 1)
    return jnp.sum(jnp.where(eye, row, jnp.zeros_like(row)), axis=1, keepdims=True)


def line(ref):
    return ref[...].reshape(1, ref.shape[0])


def fold8(t):
    return jnp.sum(t.reshape(t.shape[0] // 8, 8, t.shape[1]), axis=0)


def params(grid, vmem=VMEM_MAX):
    return pltpu.CompilerParams(dimension_semantics=("arbitrary",) * grid, vmem_limit_bytes=vmem)


def hosting(grid, ident):
    return pltpu.CompilerParams(
        dimension_semantics=("arbitrary",) * grid,
        vmem_limit_bytes=VMEM_MAX,
        collective_id=ident,
        has_side_effects=True,
    )


def sibling(index, bit):
    return index + bit - 2 * bit * (index // bit % 2)


class Place:
    def __init__(self, bits):
        self.d, self.z = lax.axis_index("dp"), lax.axis_index("tensor")
        self.core = self.d % 2
        self.a, self.b = (self.d // bit % 2 for bit in bits)
        self.spot = self.a + 2 * self.b
        self.on_core = {"dp": sibling(self.d, 1), "tensor": self.z}
        self.on_a, self.on_b = ({"dp": sibling(self.d, bit), "tensor": self.z} for bit in bits)
        peers = (None, sibling(self.z, 1), sibling(self.z, 2), sibling(sibling(self.z, 1), 2))
        self.on_z = [None] + [{"dp": self.d, "tensor": peer} for peer in peers[1:]]

    def plane(self):
        return [{"dp": (self.d + step) % 8, "tensor": self.z} for step in range(1, 8)]


def greet(targets):
    barrier = pltpu.get_barrier_semaphore()
    for target in targets:
        pl.semaphore_signal(barrier, inc=1, device_id=target, device_id_type=pl.DeviceIdType.MESH)
    pl.semaphore_wait(barrier, len(targets))


def send(src, dst, sems, at, target):
    return pltpu.make_async_remote_copy(
        src_ref=src,
        dst_ref=dst,
        send_sem=sems[0].at[at],
        recv_sem=sems[1].at[at],
        device_id=target,
        device_id_type=pl.DeviceIdType.MESH,
    )


def bits_of(dp):
    return (2, 4) if dp == 8 else (2, 8)


def chunks_of(count, tp, piece):
    cut = (piece * 5 // 8) // 8 * 8
    orders = [[1 + (j + m % 2) % (tp - 1) for j in range(tp - 1)] for m in range(count)]
    return [(m, j, *span) for m in range(count) for span in ((0, cut), (cut, piece)) for j in orders[m]]


AHEAD = 6
LAG = 2
ATTEND_COST = 0.9


class Gather:
    def __init__(self, place, chunks, mine, land, sems, publish):
        self.place, self.chunks, self.mine, self.land, self.sems, self.publish = place, chunks, mine, land, sems, publish
        self.ticks = len(chunks) + 3 * LAG
        self.got = {}

    def slot(self, k, where, low=None, high=None):
        m, j, r0, r1 = self.chunks[k]
        low, high = (r0 if low is None else low), (r1 if high is None else high)
        return self.land.at[m, j - 1, self.place.core, where, pl.ds(low, high - low)]

    def middle(self, k):
        _, _, r0, r1 = self.chunks[k]
        half = (r1 - r0) // 2
        return r0 + (half + 7 if k % 2 else half) // 8 * 8

    def over_z(self, k):
        m, j, r0, r1 = self.chunks[k]
        spots = [self.place.spot] + ([3 - self.place.spot] if j == 1 else [])
        return [
            send(self.mine.at[m, i, pl.ds(r0, r1 - r0)], self.slot(k, spot), self.sems, (k, i), self.place.on_z[j])
            for i, spot in enumerate(spots)
        ]

    def over_a(self, k):
        here = self.slot(k, self.place.spot)
        return send(here, here, self.sems, (k, 2), self.place.on_a)

    def over_b(self, k):
        here = self.slot(k, self.place.spot)
        return send(here, here, self.sems, (k, 3), self.place.on_b)

    def on_a(self, k):
        part = self.slot(k, sibling(self.place.spot, 2), None, self.middle(k))
        return send(part, part, self.sems, (k, 4), self.place.on_a)

    def on_b(self, k):
        part = self.slot(k, sibling(self.place.spot, 1), self.middle(k), None)
        return send(part, part, self.sems, (k, 5), self.place.on_b)

    def relays(self, k):
        return [] if self.chunks[k][1] == 1 else [self.on_a(k), self.on_b(k)]

    def swap(self, k):
        m, j, r0, r1 = self.chunks[k]
        part = self.land.at[m, j - 1, self.place.core, :, pl.ds(r0, r1 - r0)]
        return send(part, part, self.sems, (k, 6), self.place.on_core)

    def start_z(self, k):
        for one in self.over_z(k):
            one.start()

    def tick(self, t):
        total = len(self.chunks)
        if 0 <= t < total:
            for one in self.over_z(t):
                one.wait_recv()
            self.over_a(t).start()
            self.over_b(t).start()
            if t + AHEAD < total:
                self.start_z(t + AHEAD)
        k = t - LAG
        if 0 <= k < total:
            self.over_b(k).wait_recv()
            for one in self.relays(k)[:1]:
                one.start()
            self.over_a(k).wait_recv()
            for one in self.relays(k)[1:]:
                one.start()
        k = t - 2 * LAG
        if 0 <= k < total:
            for one in self.relays(k):
                one.wait_recv()
            self.swap(k).start()
        k = t - 3 * LAG
        if 0 <= k < total:
            self.swap(k).wait_recv()
            m, j, r0, r1 = self.chunks[k]
            piece = self.land.shape[4]
            self.got[m, j] = self.got.get((m, j), 0) + r1 - r0
            if self.got[m, j] == piece:
                self.publish(m, j, self.land[m, j - 1].reshape(8 * piece, -1).astype(BF))

    def end(self):
        for k in range(len(self.chunks)):
            for one in self.over_z(k) + self.relays(k) + [self.over_a(k), self.over_b(k), self.swap(k)]:
                one.wait_send()


def gather_scratch(count, tp, piece, width):
    total = len(chunks_of(count, tp, piece))
    return [
        pltpu.VMEM((count, tp - 1, 2, 4, piece, width), F32),
        pltpu.SemaphoreType.DMA((total, 7)),
        pltpu.SemaphoreType.DMA((total, 7)),
        pltpu.VMEM((count, 2, piece, width), F32),
    ]


class Reduce:
    def __init__(self, place, part, scratch, plan, publish):
        self.place, self.part, self.publish = place, part, publish
        self.count, self.own, self.width = part.shape
        self.out, self.half, self.first, self.second, *self.sems = scratch
        self.points = 1 + max(row[-1] for row in plan)
        self.plan = {p: [] for p in range(self.points)}
        for k, row in enumerate(plan):
            for stage, p in enumerate(row):
                self.plan[p].append((k, stage))
        for p, found in self.plan.items():
            found.sort(key=lambda one: (one[1] if p == self.points - 1 else -one[1], one[0]))
        ends = [k for p in range(self.points) for k, stage in self.plan[p] if stage == 6]
        self.closing = [max(2 * m, 2 * m + 1, key=ends.index) for m in range(self.count)]

    def greet(self):
        return [self.place.on_a, self.place.on_b, self.place.on_core]

    def rows_of(self, size, index, count):
        return pl.ds(pl.multiple_of(size * index, 8), count)

    def way(self, k):
        p = self.place
        return (p.a, p.on_a, p.b, p.on_b) if k % 2 == 0 else (p.b, p.on_b, p.a, p.on_a)

    def columns(self, bit):
        lanes = self.width // 2
        return pl.ds(pl.multiple_of(lanes * bit, LANES), lanes)

    def out_rows(self, k, bit):
        piece = self.own // 8
        return self.rows_of(piece, 4 * self.place.core + 2 * (k % 2) + bit, piece)

    def quarter(self, k, core):
        size = self.own // 4
        return self.rows_of(size, 2 * core + k % 2, size)

    def copy(self, k, stage):
        place, m, piece = self.place, k // 2, self.own // 8
        bit, peer, bit2, peer2 = self.way(k)
        if stage == 0:
            src, dst, to = self.part.at[m, self.quarter(k, 1 - place.core)], self.half.at[k], place.on_core
        elif stage == 1:
            src, dst, to = self.half.at[k, self.rows_of(piece, 1 - bit, piece)], self.first.at[k], peer
        elif stage == 2:
            src, dst, to = self.half.at[k, self.rows_of(piece, bit, piece), self.columns(1 - bit2)], self.second.at[k], peer2
        elif stage == 3:
            src = dst = self.out.at[m, self.out_rows(k, bit), self.columns(bit2)]
            to = peer2
        elif stage == 4:
            src = dst = self.out.at[m, self.out_rows(k, bit)]
            to = peer
        else:
            src = dst = self.out.at[m, self.quarter(k, place.core)]
            to = place.on_core
        return send(src, dst, self.sems, (k, stage), to)

    def step(self, k, stage):
        m, piece = k // 2, self.own // 8
        bit, _, bit2, _ = self.way(k)
        mine = self.rows_of(piece, bit, piece)
        if stage >= 1:
            self.copy(k, stage - 1).wait_recv()
        if stage == 1:
            self.half[k] = self.part[m, self.quarter(k, self.place.core)] + self.half[k]
        if stage == 2:
            self.half[k, mine] = self.half[k, mine] + self.first[k]
        if stage == 3:
            columns = self.columns(bit2)
            self.out[m, self.out_rows(k, bit), columns] = self.half[k, mine, columns] + self.second[k]
        if stage < 6:
            self.copy(k, stage).start()
            return
        if k == self.closing[m]:
            self.publish(m, self.out[m])

    def point(self, p):
        for k, stage in self.plan[p]:
            self.step(k, stage)

    def end(self):
        for k in range(2 * self.count):
            for stage in range(6):
                self.copy(k, stage).wait_send()


def reduce_scratch(count, own, width):
    chunks = 2 * count
    return [
        pltpu.VMEM((count, own, width), F32),
        pltpu.VMEM((chunks, own // 4, width), F32),
        pltpu.VMEM((chunks, own // 8, width), F32),
        pltpu.VMEM((chunks, own // 8, width // 2), F32),
        pltpu.SemaphoreType.DMA((chunks, 6)),
        pltpu.SemaphoreType.DMA((chunks, 6)),
    ]


def normalize(v):
    center = v - jnp.mean(v, axis=-1, keepdims=True)
    inv = lax.rsqrt(jnp.mean(center * center, axis=-1, keepdims=True) + EPS)
    return center * inv, inv


HEADS_IN_GROUP = 4
GROUP = HEADS_IN_GROUP * HEAD_DIM


def window_of(head):
    low = head * HEAD_DIM
    start = low // LANES * LANES
    return start, low - start


def lane_mask(offset):
    lane = lax.broadcasted_iota(jnp.int32, (1, WIN), 1)
    return (lane >= offset) & (lane < offset + HEAD_DIM)


def spread(parts):
    tiles = [None] * (GROUP // LANES)
    for head, part in enumerate(parts):
        first = window_of(head)[0] // LANES
        for half in range(WIN // LANES):
            piece = part[:, half * LANES : (half + 1) * LANES]
            at = first + half
            tiles[at] = piece if tiles[at] is None else tiles[at] + piece
    return jnp.concatenate(tiles, axis=1)


def attend_block(seq, i, q_ref, k_ref, v_ref, seg_ref, o_ref, lse_ref, bias):
    groups = q_ref.shape[1] // GROUP
    back = MAX_DOC // BLK
    here = pl.ds(pl.multiple_of(i * BLK, BLK), BLK)
    row = pl.ds(seq, 1)
    seg_col = column_of(seg_ref[row, here])

    def body(blocks):
        keys = blocks * BLK
        start = pl.multiple_of((i + 1 - blocks) * BLK, BLK)
        query = i * BLK + lax.broadcasted_iota(jnp.int32, (BLK, keys), 0)
        key = start + lax.broadcasted_iota(jnp.int32, (BLK, keys), 1)
        allowed = (query >= key) & (seg_col == seg_ref[row, pl.ds(start, keys)])
        bias[:, :keys] = jnp.where(allowed, 0.0, NEG)

        def group(gi, _):
            parts = []
            lse = lse_ref[...]
            head_lane = lax.broadcasted_iota(jnp.int32, (1, LANES), 1)
            for h in range(HEADS_IN_GROUP):
                at, off = window_of(h)
                lanes = pl.ds(pl.multiple_of(gi * GROUP + at, LANES), WIN)
                mask = lane_mask(off)
                q = q_ref[here, lanes]
                q = jnp.where(mask, q, jnp.zeros_like(q))
                t = nt(q, k_ref[pl.ds(start, keys), lanes]) * (SCALE * LOG2E) + bias[:, :keys]
                top = jnp.max(t, axis=1, keepdims=True)
                p = jnp.exp2(t - top)
                total = jnp.sum(p, axis=1, keepdims=True)
                o = nn(p.astype(BF), v_ref[pl.ds(start, keys), lanes])
                parts.append(jnp.where(mask, o * (1.0 / total), 0.0))
                lse = jnp.where(head_lane == gi * HEADS_IN_GROUP + h, top + jnp.log2(total), lse)
            lse_ref[...] = lse
            o_ref[:, pl.ds(pl.multiple_of(gi * GROUP, LANES), GROUP)] = spread(parts).astype(BF)
            return 0

        lax.fori_loop(0, groups, group, 0)

    lse_ref[...] = jnp.zeros_like(lse_ref)
    count = jnp.minimum(i, back) + 1
    for blocks in range(1, back + 2):
        pl.when(count == blocks)(functools.partial(body, blocks))


def front_kernel(
    bits, n, seqs, steps, chunks, count, x_ref, g_ref, c_ref, seg_ref, bias_ref, *refs
):
    local, refs = refs[:count], refs[count:]
    n_ref, q_ref, k_ref, v_ref, o_ref, lse_ref, vec_ref, *refs = refs
    full, refs = refs[:count], refs[count:]
    bias, weights, stage, qs, ks, vs, ns, passing, fresh, land, gather_s, gather_r, mine, raw, bias_in, bias_s, bias_r, local_sem, out_sem, raw_sem, copy_sem, back_sem = refs
    own = local[0].shape[0]
    held_here = weights.shape[0]
    step = pl.program_id(0)
    place = Place(bits)
    shards_ = len(place.on_z)
    ahead = 2 * n + (seqs - 1) * n
    order = {}

    def rows_of(j):
        return pl.ds(j * own, own)

    def stage_copy(number):
        m, j = order[number]
        return pltpu.make_async_copy(stage.at[number % 2], full[m].at[rows_of(j)], out_sem.at[number])

    def publish(m, j, shard):
        if m < held_here:
            weights[m, rows_of(j)] = shard
            return
        number = len(order)
        order[number] = m, j
        if number >= 2:
            stage_copy(number - 2).wait()
        stage[number % 2] = shard
        stage_copy(number).start()

    work = Gather(place, chunks, mine, land, (gather_s, gather_r), publish)
    ready = [max(k for k, chunk in enumerate(chunks) if chunk[0] == m) + 3 * LAG + 1 for m in range(held_here)]

    def own_copies():
        held_ = [pltpu.make_async_copy(local[m], weights.at[m, rows_of(0)], local_sem.at[m]) for m in range(held_here)]
        rest = [
            pltpu.make_async_copy(local[m], full[m].at[rows_of(0)], local_sem.at[m]) for m in range(held_here, count)
        ]
        return held_, rest

    def held_out():
        return [pltpu.make_async_copy(weights.at[m], full[m], local_sem.at[m]) for m in range(held_here)]

    @pl.when(step == 0)
    def _():
        held_, rest = own_copies()
        piece = own // 8
        raws = [
            [
                pltpu.make_async_copy(
                    local[m].at[pl.ds(pl.multiple_of(piece * (4 * place.core + spot), 8), piece)],
                    raw.at[m % 2, i],
                    raw_sem.at[m % 2, i],
                )
                for i, spot in enumerate((place.spot, 3 - place.spot))
            ]
            for m in range(count)
        ]
        for one in sum(raws[:2], []) + held_ + rest:
            one.start()
        greet(place.on_z[1:] + [place.on_a, place.on_b, place.on_core])
        for m in range(count):
            for i, one in enumerate(raws[m]):
                one.wait()
                mine[m, i] = raw[m % 2, i].astype(F32)
            for one in raws[m + 2] if m + 2 < count else []:
                one.start()
            if m == 0:
                for k in range(AHEAD):
                    work.start_z(k)
        vectors = [
            send(bias_ref.at[j], bias_in.at[j], (bias_s, bias_r), j, place.on_z[j]) for j in range(1, shards_)
        ]
        for one in vectors:
            one.start()
        for t in range(ready[0]):
            work.tick(t)
        for one in vectors:
            one.wait()
        vec_ref[...] = sum((bias_in[j] for j in range(1, shards_)), bias_ref[0])
        for one in held_:
            one.wait()

    @pl.when(step == 1 + ahead)
    def _():
        for one in held_out():
            one.start()

    unit = jnp.maximum(step - 1 - ahead, 0)
    seq, part = unit // (2 * n), unit % (2 * n)
    early = jnp.maximum(step - 1 - 2 * n, 0)
    block = jnp.where(step <= 2 * n, (step - 1 + n) % n, jnp.where(step <= ahead, early % n, part % n))
    here = pl.ds(pl.multiple_of(block * BLK, BLK), BLK)

    def leave(i, src, dst, sequence):
        there = pl.ds(pl.multiple_of((sequence * n + block) * BLK, BLK), BLK)
        return pltpu.make_async_copy(src, dst.at[there], copy_sem.at[i, block])

    def enter(sequence):
        there = pl.ds(pl.multiple_of(sequence * n * BLK, BLK), n * BLK)
        return [
            pltpu.make_async_copy(src.at[there], dst, back_sem.at[i]) for i, (src, dst) in enumerate(((q_ref, qs), (k_ref, ks)))
        ]

    first = (step > 0) & (step <= n)
    second = (step > n) & (step <= 2 * n)
    passing_by = (step > 2 * n) & (step <= ahead)
    third = (step > ahead) & (part < n)
    again = third & (seq > 0)

    @pl.when(again)
    def _():
        @pl.when(part == 0)
        def _():
            for one in enter(seq):
                one.start()

        leave(2, ns.at[here], n_ref, seq - 1).wait()
        leave(3, vs.at[here], v_ref, seq - 1).wait()

    @pl.when(first | passing_by | again)
    def _():
        hat, _ = normalize(x_ref[...].astype(F32))
        fresh[...] = (hat * line(g_ref) + line(c_ref)).astype(BF)

    @pl.when(first | again)
    def _():
        ns[here] = fresh[...]

    @pl.when(second | (third & (seq == 0)))
    def _():
        fresh[...] = ns[here]

    @pl.when(first | second | passing_by | third)
    def _():
        low = jnp.where(third, 2, jnp.where(second, 1, 0))

        def make(m, carry):
            row = jnp.where(m == 0, 0, jnp.where(m == 1, 3, 1))
            passing[m % 2] = (nt(fresh[...], weights[m]) + vec_ref[pl.ds(row, 1)]).astype(BF)
            return carry

        lax.fori_loop(low, low + jnp.where(passing_by, 2, 1), make, 0)

    @pl.when(first)
    def _():
        qs[here] = passing[0]
        leave(0, qs.at[here], q_ref, 0).start()
        leave(2, ns.at[here], n_ref, 0).start()

    @pl.when(second)
    def _():
        ks[here] = passing[1]
        leave(1, ks.at[here], k_ref, 0).start()

    @pl.when(passing_by)
    def _():
        copies = [leave(3 + i, passing.at[i], dst, 1 + early // n) for i, dst in enumerate((q_ref, k_ref))]
        for one in copies:
            one.start()
        for one in copies:
            one.wait()

    @pl.when(third)
    def _():
        vs[here] = passing[0]
        leave(3, vs.at[here], v_ref, seq).start()

    @pl.when(again)
    def _():
        leave(2, ns.at[here], n_ref, seq).start()

        @pl.when(part == n - 1)
        def _():
            for one in enter(seq):
                one.wait()

    @pl.when((step > ahead) & (part == n) & (seq == 0))
    def _():
        for b in range(n):
            there = pl.ds(b * BLK, BLK)
            pltpu.make_async_copy(qs.at[there], q_ref.at[there], copy_sem.at[0, b]).wait()
            pltpu.make_async_copy(ks.at[there], k_ref.at[there], copy_sem.at[1, b]).wait()

    @pl.when((step > ahead) & (part >= n))
    def _():
        attend_block(seq, part - n, qs, ks, vs, seg_ref, o_ref, lse_ref, bias)

    reach = MAX_DOC // BLK + 1
    attention = [min(i + 1, reach) * ATTEND_COST for i in range(n)]
    lengths = [1.0] * (ahead + 1) + [1.0] * n + attention + ([1.6] * n + attention) * (seqs - 1)
    starts = (1, 1 + n, 1 + ahead, steps)
    for t in range(ready[0], work.ticks):
        m = sum(t >= one for one in ready)
        first, upto = ready[m - 1], (ready + [work.ticks])[m]
        span = lengths[starts[m - 1] : starts[m]]
        goal, at, passed = (t - first + 1) / (upto - first) * sum(span), starts[m - 1], span[0]
        while passed < goal - 1e-6 and at < starts[m] - 1:
            at += 1
            passed += lengths[at]
        pl.when(step == at)(functools.partial(work.tick, t))

    @pl.when(step == steps - 1)
    def _():
        work.end()
        for number in range(max(0, len(order) - 2), len(order)):
            stage_copy(number).wait()
        for one in held_out() + own_copies()[1]:
            one.wait()
        for b in range(n):
            for i, (src, dst) in ((2, (ns, n_ref)), (3, (vs, v_ref))):
                there = pl.ds(((seqs - 1) * n + b) * BLK, BLK)
                pltpu.make_async_copy(src.at[pl.ds(b * BLK, BLK)], dst.at[there], copy_sem.at[i, b]).wait()


def front(x, g1, c1, seg, biases, shards_, dp, tp):
    tokens, width = x.shape
    seqs, length = seg.shape
    n = length // BLK
    count, own = len(shards_), shards_[0].shape[0]
    bits, piece, steps, out = bits_of(dp), own // 8, 1 + 2 * n + (seqs - 1) * n + 2 * seqs * n, tp * own
    chunks = chunks_of(count, tp, piece)

    ahead = 2 * n + (seqs - 1) * n

    def unit(i):
        return jnp.maximum(i - 1 - ahead, 0)

    def early(i):
        opening = jnp.minimum(jnp.maximum(i - 1, 0), n - 1)
        later = n + jnp.maximum(i - 1 - 2 * n, 0)
        again = unit(i) // (2 * n) * n + jnp.minimum(unit(i) % (2 * n), n - 1)
        return (jnp.where(i <= 2 * n, opening, jnp.where(i <= ahead, later, jnp.where(unit(i) < 2 * n, ahead - n - 1, again))), 0)

    def late(size):
        return pl.BlockSpec((BLK, size), lambda i: (unit(i) // (2 * n) * n + jnp.maximum(unit(i) % (2 * n) - n, 0), 0))

    anywhere = pl.BlockSpec(memory_space=pl.ANY)
    pairs = seqs * n * 2.5 * BLK * BLK * (out // HEAD_DIM)
    return pl.pallas_call(
        functools.partial(front_kernel, bits, n, seqs, steps, chunks, count),
        grid=(steps,),
        in_specs=[
            pl.BlockSpec((BLK, width), early),
            whole(g1.shape),
            whole(c1.shape),
            whole(seg.shape),
            whole(biases.shape),
        ]
        + [anywhere] * count,
        out_specs=[anywhere] * 4 + [late(out), late(LANES), held(biases.shape[1:])] + [anywhere] * count,
        out_shape=[jax.ShapeDtypeStruct((tokens, width), BF)]
        + [jax.ShapeDtypeStruct((tokens, out), BF)] * 4
        + [jax.ShapeDtypeStruct((tokens, LANES), F32), jax.ShapeDtypeStruct(biases.shape[1:], F32)]
        + [jax.ShapeDtypeStruct((out, width), BF)] * count,
        scratch_shapes=[
            pltpu.VMEM((BLK, BLK + MAX_DOC), F32),
            pltpu.VMEM((3, out, width), BF),
            pltpu.VMEM((2, own, width), BF),
        ]
        + [pltpu.VMEM((length, out), BF)] * 3
        + [pltpu.VMEM((length, width), BF), pltpu.VMEM((2, BLK, out), BF), pltpu.VMEM((BLK, width), BF)]
        + gather_scratch(count, tp, piece, width)
        + [
            pltpu.VMEM((2, 2, piece, width), BF),
            pltpu.VMEM(biases.shape, F32),
            pltpu.SemaphoreType.DMA((tp,)),
            pltpu.SemaphoreType.DMA((tp,)),
            pltpu.SemaphoreType.DMA((count,)),
            pltpu.SemaphoreType.DMA((count * tp,)),
            pltpu.SemaphoreType.DMA((2, 2)),
            pltpu.SemaphoreType.DMA((5, n)),
            pltpu.SemaphoreType.DMA((2,)),
        ],
        compiler_params=hosting(1, 0),
        cost_estimate=pl.CostEstimate(
            flops=int(6 * tokens * width * out + pairs * 8 * WIN),
            bytes_accessed=12 * tokens * width + 4 * count * out * width,
            transcendentals=int(pairs),
        ),
        name="front",
    )(x, g1, c1, seg, biases, *shards_)


def attend_back_kernel(
    steps, bits, q_ref, do_ref, o_ref, lse_ref, k_ref, v_ref, seg_ref, part_ref, dq_ref, dk_ref, dv_ref, go_ref, g1_ref, g2_ref,
    bias, dq_acc, lse_t, delta_t, *reduce_refs,
):
    s, j = pl.program_id(0), pl.program_id(1)
    n = pl.num_programs(1)
    length, width = q_ref.shape
    groups = width // GROUP
    ahead = MAX_DOC // BLK

    step = s * n + j

    def publish(m, total):
        (go_ref, g1_ref, g2_ref)[m][...] = total

    if bits is not None:
        work = Reduce(Place(bits), part_ref, reduce_refs, BACK_PLAN, publish)

        @pl.when(step == 0)
        def _():
            greet(work.greet())
            work.point(0)

    @pl.when(j == 0)
    def _():
        dq_acc[...] = jnp.zeros_like(dq_acc)
        head = lax.broadcasted_iota(jnp.int32, (16, width), 0)
        lane = lax.broadcasted_iota(jnp.int32, (16, width), 1)
        pick = jnp.where((lane >= head * HEAD_DIM) & (lane < (head + 1) * HEAD_DIM), 1.0, 0.0).astype(BF)
        for b in range(length // BLK):
            at = slice(b * BLK, (b + 1) * BLK)
            lse_t[:, at] = lse_ref[at, :].T[:16, :]
            prod = do_ref[at, :].astype(F32) * o_ref[at, :].astype(F32)
            high = prod.astype(BF)
            rest = (prod - high.astype(F32)).astype(BF)
            delta_t[:, at] = nt(pick, high) + nt(pick, rest)

    count = jnp.minimum(n - j, ahead + 1)
    start = pl.multiple_of(j * BLK, BLK)
    seg_col = column_of(seg_ref[pl.ds(s, 1), pl.ds(start, BLK)])

    def mask_of(blocks):
        queries = blocks * BLK
        row = lax.broadcasted_iota(jnp.int32, (BLK, queries), 0)
        col = lax.broadcasted_iota(jnp.int32, (BLK, queries), 1)
        allowed = (row <= col) & (seg_col == seg_ref[pl.ds(s, 1), pl.ds(start, queries)])
        bias[:, :queries] = jnp.where(allowed, 0.0, NEG)

    def heads(gi, blocks):
        queries = blocks * BLK
        span = pl.ds(start, queries)
        dks, dvs = [], []
        for h in range(HEADS_IN_GROUP):
            at, off = window_of(h)
            lanes = pl.ds(pl.multiple_of(gi * GROUP + at, LANES), WIN)
            mask = lane_mask(off)
            head = pl.ds(gi * HEADS_IN_GROUP + h, 1)
            k = k_ref[:, lanes]
            k = jnp.where(mask, k, jnp.zeros_like(k))
            v = v_ref[:, lanes]
            v = jnp.where(mask, v, jnp.zeros_like(v))
            q = q_ref[span, lanes]
            do = do_ref[span, lanes]
            t = nt(k, q) * (SCALE * LOG2E) + bias[:, :queries]
            p = jnp.exp2(t - lse_t[head, span])
            dvs.append(jnp.where(mask, nn(p.astype(BF), do), 0.0))
            ds = (p * (nt(v, do) - delta_t[head, span])).astype(BF)
            dks.append(jnp.where(mask, nn(ds, q), 0.0))
            dq_acc[span, lanes] += tn(ds, k)
        out = pl.ds(pl.multiple_of(gi * GROUP, LANES), GROUP)
        dk_ref[:, out] = (spread(dks) * SCALE).astype(BF)
        dv_ref[:, out] = spread(dvs).astype(BF)

    kinds = range(1, ahead + 2)
    for blocks in kinds:
        pl.when(count == blocks)(functools.partial(mask_of, blocks))

    def group(gi, carry):
        for blocks in kinds:
            pl.when(count == blocks)(functools.partial(heads, gi, blocks))
        if bits is not None:
            for p in range(1, work.points):
                pl.when(step * groups + gi + 1 == p)(functools.partial(work.point, p))
        return carry

    lax.fori_loop(0, groups, group, 0)

    if bits is not None:
        pl.when(step == steps - 1)(work.end)
    else:
        for m in range(3):
            publish(m, part_ref[m])

    @pl.when(j == n - 1)
    def _():
        dq_ref[...] = (dq_acc[...] * SCALE).astype(BF)


def attend_back(q, k, v, seg, mixed, d_mixed, lse, parts, bits):
    tokens, width = q.shape
    seqs, length = seg.shape
    own, model = parts.shape[1:]
    n = length // BLK
    spec_k = pl.BlockSpec((BLK, width), lambda s, j: (s * n + j, 0))
    spec_q = pl.BlockSpec((length, width), lambda s, j: (s, 0))
    pairs = seqs * n * 2.5 * BLK * BLK * (width // HEAD_DIM)
    hosted = bits is not None
    return pl.pallas_call(
        functools.partial(attend_back_kernel, seqs * n, bits),
        grid=(seqs, n),
        in_specs=[
            spec_q,
            spec_q,
            spec_q,
            pl.BlockSpec((length, LANES), lambda s, j: (s, 0)),
            spec_k,
            spec_k,
            whole(seg.shape),
            whole(parts.shape),
        ],
        out_specs=[spec_q, spec_k, spec_k] + [held((own, model))] * 3,
        scratch_shapes=[
            pltpu.VMEM((BLK, BLK + MAX_DOC), F32),
            pltpu.VMEM((length, width), F32),
            pltpu.VMEM((16, length), F32),
            pltpu.VMEM((16, length), F32),
        ]
        + (reduce_scratch(*parts.shape) if hosted else []),
        out_shape=[jax.ShapeDtypeStruct((tokens, width), BF)] * 3 + [jax.ShapeDtypeStruct((own, model), F32)] * 3,
        compiler_params=hosting(2, 3) if hosted else params(2),
        cost_estimate=pl.CostEstimate(
            flops=int(pairs * 20 * WIN), bytes_accessed=16 * tokens * width, transcendentals=int(pairs)
        ),
        name="attend_back",
    )(q, d_mixed, mixed, lse, k, v, seg, parts)


BACK_PLAN = (
    (0, 1, 4, 7, 9, 11, 14),
    (0, 2, 4, 6, 10, 13, 14),
    (1, 2, 5, 8, 10, 13, 14),
    (0, 1, 3, 8, 11, 14, 16),
    (0, 5, 9, 10, 13, 15, 16),
    (0, 3, 6, 11, 13, 15, 16),
)
FINISH_PLAN = (
    (0, 1, 6, 10, 13, 19, 26),
    (0, 1, 5, 9, 13, 18, 21),
    (5, 6, 12, 16, 19, 24, 26),
    (1, 3, 10, 17, 21, 25, 26),
    (2, 3, 9, 17, 20, 25, 26),
    (4, 5, 12, 16, 19, 23, 25),
)

OWN_ROW = 6


def middle_kernel(
    own, m_ref, x_ref, g_ref, w_ref, wo_ref, w1_ref, w2_ref, bo_ref, g2_ref, c2_ref, b2_ref, b1_ref,
    y_ref, dr_ref, dm_ref, part_ref, small_ref, rms_ref, vec, sums,
):
    i = pl.program_id(0)

    @pl.when(i == 0)
    def _():
        part_ref[...] = jnp.zeros_like(part_ref)
        vec[...] = jnp.zeros_like(vec)
        sums[...] = jnp.zeros_like(sums)

    mixed = m_ref[...]
    cot = g_ref[...]
    attended = nn(mixed, wo_ref[...]) + line(bo_ref)
    resid = x_ref[...].astype(F32) + attended
    hat, inv = normalize(resid)
    normed = (hat * line(g2_ref) + line(c2_ref)).astype(BF)
    pre = nt(normed, w1_ref[...]) + b1_ref[2:3]
    cdf = 0.5 + 0.5 * lax.erf(pre * math.sqrt(0.5))
    act = (pre * cdf).astype(BF)
    slope = cdf + pre * jnp.exp(-0.5 * pre * pre) * (1.0 / math.sqrt(2.0 * math.pi))
    branch = nn(act, w2_ref[...]) + line(b2_ref)
    output = resid + branch
    y_ref[...] = output.astype(BF)
    per = w_ref.shape[1] // BLK
    seq, at_ = i // per, i % per
    valid = w_ref[pl.ds(seq, 1), pl.ds(pl.multiple_of(at_ * BLK, BLK), BLK)].astype(F32)
    weight = column_of(valid)
    lane = lax.broadcasted_iota(jnp.int32, (1, LANES), 1)
    found = jnp.where(lane == 3, jnp.sum(valid, axis=1, keepdims=True), 0.0)
    for at, v in enumerate((attended, branch, output)):
        one = jnp.sum(weight * jnp.sum(v * v, axis=1, keepdims=True), axis=0, keepdims=True)
        found = jnp.where(lane == at, one, found)
    at_row = lax.broadcasted_iota(jnp.int32, sums.shape, 0) == seq
    sums[...] += jnp.where(at_row, found, 0.0)

    d_pre = (nt(cot, w2_ref[...]) * slope).astype(BF)
    part_ref[2] += tn(act[:, :own], cot)
    part_ref[1] += tn(d_pre[:, :own], normed)
    d_normed = nn(d_pre, w1_ref[...])
    d_hat = d_normed * line(g2_ref)
    grad = cot.astype(F32)
    d_resid = grad + inv * (
        d_hat - jnp.mean(d_hat, axis=1, keepdims=True) - hat * jnp.mean(d_hat * hat, axis=1, keepdims=True)
    )
    dr_ref[...] = d_resid
    low = d_resid.astype(BF)
    part_ref[0] += tn(mixed[:, :own], low)
    dm_ref[...] = nt(low, wo_ref[...]).astype(BF)
    for at, v in enumerate((grad, d_normed * hat, d_normed, low.astype(F32), d_pre.astype(F32))):
        vec[at] += fold8(v)

    @pl.when(i == pl.num_programs(0) - 1)
    def _():
        total = sums[...]
        counted = jnp.sum(jnp.where(lane == 3, total, 0.0), axis=1, keepdims=True)
        each = jnp.sqrt(total / (jnp.maximum(counted, 1.0) * attended.shape[1]))
        rms_ref[...] = each[: rms_ref.shape[0], : rms_ref.shape[1]]
        small_ref[...] = jnp.zeros_like(small_ref)
        for at, row in enumerate((0, 1, 2, 3, OWN_ROW)):
            small_ref[row : row + 1] = jnp.sum(vec[at], axis=0, keepdims=True)


def middle(own, mixed, x, cot, valid, wo, w1, w2, bo, g2, c2, b2, b1):
    tokens, width = x.shape
    inner, hidden = wo.shape[0], w1.shape[0]
    n = tokens // BLK
    return pl.pallas_call(
        functools.partial(middle_kernel, own),
        grid=(n,),
        in_specs=[rows(inner), rows(width), rows(width), whole(valid.shape)]
        + [whole((inner, width)), whole((hidden, width)), whole((hidden, width))]
        + [whole((width,))] * 4
        + [whole(b1.shape)],
        out_specs=[
            rows(width),
            rows(width),
            rows(inner),
            held((3, own, width)),
            held((8, width)),
            held((valid.shape[0], 3)),
        ],
        out_shape=[
            jax.ShapeDtypeStruct((tokens, width), BF),
            jax.ShapeDtypeStruct((tokens, width), F32),
            jax.ShapeDtypeStruct((tokens, inner), BF),
            jax.ShapeDtypeStruct((3, own, width), F32),
            jax.ShapeDtypeStruct((8, width), F32),
            jax.ShapeDtypeStruct((valid.shape[0], 3), F32),
        ],
        scratch_shapes=[pltpu.VMEM((5, 8, width), F32), pltpu.VMEM((-(-valid.shape[0] // 8) * 8, LANES), F32)],
        compiler_params=params(1),
        cost_estimate=pl.CostEstimate(
            flops=2 * tokens * width * (6 * width + 3 * own),
            bytes_accessed=14 * tokens * width + 6 * width * width,
            transcendentals=2 * tokens * hidden,
        ),
        name="middle",
    )(mixed, x, cot, valid, wo, w1, w2, bo, g2, c2, b2, b1)


def finish_kernel(
    bits, own, steps, dq_ref, dk_ref, dv_ref, x_ref, dr_ref, g_ref, wq_ref, wk_ref, wv_ref, mq_ref, mk_ref, mv_ref, n_ref, in_ref,
    dx_ref, gq_ref, gk_ref, gv_ref, small_ref, vec, part, acc, taken, *refs,
):
    step = pl.program_id(0)
    grads = (mq_ref, mk_ref, mv_ref)
    count = len(grads)
    half = part.shape[2] // 2

    def publish(m, total):
        (gq_ref, gk_ref, gv_ref)[m][...] = total

    if bits is not None:
        place = Place(bits)
        work = Reduce(place, part, refs[:-3], FINISH_PLAN, publish)
        box, *sems = refs[-3:]

    @pl.when(step == 0)
    def _():
        vec[...] = jnp.zeros_like(vec)
        small_ref[...] = in_ref[...]
        if bits is not None:
            greet(place.plane())

    def take(m):
        taken[...] = grads[m][...]

    for m in range(count):
        pl.when(step == m)(functools.partial(take, m))

    @pl.when(step < count)
    def _():
        mine = taken[:, :own]
        part[step] = tn(mine, n_ref[...])
        total = jnp.sum(mine.astype(F32), axis=0, keepdims=True)
        for m in (0, 2):

            @pl.when(step == m)
            def _(at=m // 2 * half):
                small_ref[OWN_ROW + 1 : OWN_ROW + 2, at : at + own] = total

    def points(first, at, every):
        if bits is not None:
            for p in range(first, work.points, every):
                if work.plan[p]:
                    pl.when(step == at + (p - first) // every)(functools.partial(work.point, p))

    if bits is not None:
        for m in range(count):
            pl.when(step == m)(functools.partial(work.point, m))

    @pl.when(step >= count)
    def _():
        acc[...] = nn(dq_ref[...], wq_ref[...])
        points(count, count, 3)
        acc[...] += nn(dk_ref[...], wk_ref[...])
        points(count + 1, count, 3)
        d_normed = acc[...] + nn(dv_ref[...], wv_ref[...])
        hat, inv = normalize(x_ref[...].astype(F32))
        d_hat = d_normed * line(g_ref)
        dx_ref[...] = dr_ref[...] + inv * (
            d_hat - jnp.mean(d_hat, axis=1, keepdims=True) - hat * jnp.mean(d_hat * hat, axis=1, keepdims=True)
        )
        vec[0] += fold8(d_normed * hat)
        vec[1] += fold8(d_normed)
        points(count + 2, count, 3)

    @pl.when(step == steps - 1)
    def _():
        for at in range(2):
            small_ref[4 + at : 5 + at] = jnp.sum(vec[at], axis=0, keepdims=True)
        if bits is None:
            for m in range(count):
                publish(m, part[m])
        else:
            copies = [send(small_ref, box.at[place.d], sems, i, peer) for i, peer in enumerate(place.plane())]
            for one in copies:
                one.start()
            box[place.d] = small_ref[...]
            for one in copies:
                one.wait_recv()
            for one in copies:
                one.wait_send()
            total = box[0]
            for i in range(1, 8):
                total = total + box[i]
            small_ref[...] = total
            work.end()


def finish(dq, dk, dv, x, d_resid, g1, wq, wk, wv, normed1, small, own, bits):
    tokens, width = x.shape
    inner = wq.shape[0]
    hosted = bits is not None
    count = 3
    pad = -(-own // LANES) * LANES
    mine = pl.BlockSpec((tokens, pad), lambda i: (0, 0), pipeline_mode=pl.Buffered(1))

    def late(size):
        return pl.BlockSpec((BLK, size), lambda i: (jnp.maximum(i - count, 0), 0))

    return pl.pallas_call(
        functools.partial(finish_kernel, bits, own, count + tokens // BLK),
        grid=(count + tokens // BLK,),
        in_specs=[late(inner)] * 3
        + [late(width), late(width), whole((width,))]
        + [whole((inner, width))] * 3
        + [mine] * 3
        + [whole((tokens, width)), whole((8, width))],
        out_specs=[late(width)] + [held((own, width))] * 3 + [held((8, width))],
        out_shape=[jax.ShapeDtypeStruct((tokens, width), F32)]
        + [jax.ShapeDtypeStruct((own, width), F32)] * 3
        + [jax.ShapeDtypeStruct((8, width), F32)],
        scratch_shapes=[
            pltpu.VMEM((2, 8, width), F32),
            pltpu.VMEM((count, own, width), F32),
            pltpu.VMEM((BLK, width), F32),
            pltpu.VMEM((tokens, pad), BF),
        ]
        + (
            reduce_scratch(count, own, width)
            + [pltpu.VMEM((8, 8, width), F32), pltpu.SemaphoreType.DMA((7,)), pltpu.SemaphoreType.DMA((7,))]
            if hosted
            else []
        ),
        compiler_params=hosting(1, 4) if hosted else params(1),
        cost_estimate=pl.CostEstimate(
            flops=6 * tokens * width * inner, bytes_accessed=16 * tokens * width + 6 * width * inner, transcendentals=0
        ),
        name="finish",
    )(dq, dk, dv, x, d_resid, g1, wq, wk, wv, dq, dk, dv, normed1, small)


def shards(dp, tp, x, g1, c1, wq, bq, wk, wv, bv, wo, bo, g2, c2, w1, b1, w2, b2, seg, valid, cot):
    tokens, width = x.shape
    seqs, length = seg.shape
    own = wq.shape[1]
    bits = bits_of(dp) if dp == 8 else None

    own_biases = jnp.stack([bq, bv, b1])
    own_biases = jnp.concatenate([jnp.tile(own_biases, (1, tp)), jnp.zeros((5, tp * own), F32)], axis=0)
    place = lax.broadcasted_iota(jnp.int32, (tp, 8, tp * own), 2) // own
    biases = jnp.where(place == lax.broadcasted_iota(jnp.int32, place.shape, 0), own_biases[None], 0.0)
    normed1, q, k, v, mixed, lse, vectors, fq, fk, fv, fo, f1, f2 = front(
        x, g1, c1, seg, biases, [wq.T, wk.T, wv.T, wo, w1.T, w2], dp, tp
    )

    y, d_resid, d_mixed, parts, small, rms = middle(
        own, mixed, x, cot, valid, fo, f1, f2, bo, g2, c2, b2, vectors
    )
    dq, dk, dv, gwo, gw1, gw2 = attend_back(q, k, v, seg, mixed, d_mixed, lse, parts, bits)
    grad_input, gq, gk, gv, small = finish(dq, dk, dv, x, d_resid, g1, fq, fk, fv, normed1, small, own, bits)
    if bits is None:
        gwo, gw1, gw2, gq, gk, gv, small = lax.psum((gwo, gw1, gw2, gq, gk, gv, small), "dp")

    gb2, gg2, gc2, gbo, gg1, gc1 = (small[r] for r in range(6))
    gb1 = small[OWN_ROW, :own]
    gbq = small[OWN_ROW + 1, :own]
    gbv = small[OWN_ROW + 1, width // 2 : width // 2 + own]
    return (y, grad_input, gg1, gc1, gq.T, gbq, gk.T, gv.T, gbv, gwo, gbo, gg2, gc2, gw1.T, gb1, gw2, gb2, rms)


def solution(mesh):
    dp, tp = mesh.shape["dp"], mesh.shape["tensor"]
    tok, col, row, vec, rep = P("dp", None), P(None, "tensor"), P("tensor", None), P("tensor"), P()
    return jax.shard_map(
        functools.partial(shards, dp, tp),
        mesh=mesh,
        in_specs=(tok, rep, rep, col, vec, col, col, vec, row, rep, rep, rep, col, vec, row, rep, tok, tok, tok),
        out_specs=(tok, tok, rep, rep, col, vec, col, col, vec, row, rep, rep, rep, col, vec, row, rep, tok),
        check_vma=False,
    )
```

profile of v0, /device:TPU:0, one launch (start us, length us, event | category | flops | bytes accessed | tf_op | source)
XLA Modules:
  0.0 378.9 jit_solution(12113785299505523504)
XLA Ops:
  0.7 0.7 stack.12
  1.3 0.7 stack.13
  2.0 0.7 stack.14
  2.7 0.1 tile.10
  2.9 0.7 fusion.bias_ref
  3.6 156.1 %front.1 = (bf16[2048,1280]{1,0:T(8,128)(2,1)}, bf16[2048,1280]{1,0:T(8,128)(2,1)}, bf16[2048,1280]{1,0:T(8,128)(2,1)}, bf16[2048,1280]{1,0:T(8,128)(2,1)}, bf16...) custom-call(bf16[2048,1280]{1,0:T(8,128)(2,1)} %x_ref.5, ...), custom_call_target="tpu_custom_call" | custom-call | flops 41607495680 | bytes 70778880 | tf_op jit(solution)/shard_map/front/pallas_call | solution.py:643
  159.7 69.4 %middle.1 = (bf16[2048,1280]{1,0:T(8,128)(2,1)}, f32[2048,1280]{1,0:T(8,128)}, bf16[2048,1280]{1,0:T(8,128)(2,1)}, f32[3,320,1280]{2,1,0:T(8,128)}, f32[8,1280]{1,0:T(8,128)}, /*index=5*/f32[2,3]{1,0:T(2,128)}) custom-call(bf16[2048,1280]{1,0:T(8,128)(2,1)} %get-tuple-element.48.m_ref.o_ref, bf16[2048,1280]{1,0:T(8,128)(2,1)} %x_ref.5, ...), custom_call_target="tpu_custom_call" | custom-call | flops 45298483200 | bytes 46530560 | tf_op jit(solution)/shard_map/middle/pallas_call | solution.py:913
  229.0 61.8 %attend_back.1 = (bf16[2048,1280]{1,0:T(8,128)(2,1)}, bf16[2048,1280]{1,0:T(8,128)(2,1)}, bf16[2048,1280]{1,0:T(8,128)(2,1)}, f32[320,1280]{1,0:T(8,128)}, f32[320,1280]{1,0:T(8,128)}, /*index=5*/f32[320,1280]{1,0:T(8,128)}) custom-call(bf16[2048,1280]{1,0:T(8,128)(2,1)} %get-tuple-element.54.q_ref, bf16[2048,1280]{1,0:T(8,128)(2,1)} %get-tuple-element.55.do_ref, ...), custom_call_target="tpu_custom_call" | custom-call | flops 53687091200 | bytes 41943040 | tf_op jit(solution)/shard_map/attend_back/pallas_call | solution.py:795
  290.9 68.1 %finish.1 = (f32[2048,1280]{1,0:T(8,128)}, f32[320,1280]{1,0:T(8,128)}, f32[320,1280]{1,0:T(8,128)}, f32[320,1280]{1,0:T(8,128)}, f32[8,1280]{1,0:T(8,128)}) custom-call(bf16[2048,1280]{1,0:T(8,128)(2,1)} %get-tuple-element.60.dq_ref.mq_ref, bf16[2048,1280]{1,0:T(8,128)(2,1)} %get-tuple-element.61.dk_ref.mk_ref, ...), custom_call_target="tpu_custom_call" | custom-call | flops 20132659200 | bytes 51773440 | tf_op jit(solution)/shard_map/finish/pallas_call | solution.py:1048
  359.0 1.4 slice_reduce_fusion.6
  360.3 1.8 slice_reduce_fusion
  362.1 8.9 %copy.44 = f32[2048,1280]{1,0:T(8,128)} copy(f32[2048,1280]{1,0:T(8,128)} %get-tuple-element.108) | data formatting | bytes 20971520
  371.0 0.0 copy-done.5
  371.0 1.2 copy.45
  372.2 0.9 copy-done.4
  373.0 1.2 copy.46
  374.2 0.0 copy-done.3
  374.2 1.2 copy.47
  375.3 0.0 copy-done.2
  375.4 1.2 copy.48
  376.5 0.0 copy-done.1
  376.5 1.2 copy.49
  377.7 0.0 copy-done
  377.7 1.2 copy.50
  (11 shorter events, 0.1 us)
Async XLA Ops:
  362.1 8.9 %copy-start.5 = (f32[320,1280]{1,0:T(8,128)S(1)}, f32[320,1280]{1,0:T(8,128)}, u32[]{:S(2)}) copy-start(f32[320,1280]{1,0:T(8,128)} %get-tuple-element.71) | copy-start | bytes 4915204
  371.0 2.0 copy-start.4
  371.0 3.2 copy-start.3
  373.0 2.3 copy-start.2
  374.2 2.3 copy-start.1
  375.4 2.3 copy-start
where the time goes:
time: 379 us
  Pallas kernels  355 us (94%)
  local copies, waits for them, and re-layouts  22 us (6%)
    pallas_call x1, Pallas kernels, front(): pl.pallas_call(functools.partial(front_kernel, bits, n, seqs, steps, chun...  156 us
    pallas_call x1, Pallas kernels, middle(): pl.pallas_call(functools.partial(middle_kernel, own), grid=(n,), in_specs...  69.4 us
    pallas_call x1, Pallas kernels, finish(): pl.pallas_call(functools.partial(finish_kernel, bits, own, count + tokens...  68.1 us
    pallas_call x1, Pallas kernels, attend_back(): pl.pallas_call(functools.partial(attend_back_kernel, seqs * n, bits), gri...  61.8 us
    unnamed x19, local copies, waits for them, and re-layouts  16.7 us

commit v1 on v0

--- a/solution.py
+++ b/solution.py
@@ -129,7 +129,7 @@
     def __init__(self, place, chunks, mine, land, sems, publish):
         self.place, self.chunks, self.mine, self.land, self.sems, self.publish = place, chunks, mine, land, sems, publish
         self.ticks = len(chunks) + 3 * LAG
-        self.got = {}
+        self.closing = {(m, j): k for k, (m, j, _, _) in enumerate(chunks)}
 
     def slot(self, k, where, low=None, high=None):
         m, j, r0, r1 = self.chunks[k]
@@ -202,10 +202,9 @@
         k = t - 3 * LAG
         if 0 <= k < total:
             self.swap(k).wait_recv()
-            m, j, r0, r1 = self.chunks[k]
-            piece = self.land.shape[4]
-            self.got[m, j] = self.got.get((m, j), 0) + r1 - r0
-            if self.got[m, j] == piece:
+            m, j, _, _ = self.chunks[k]
+            if self.closing[m, j] == k:
+                piece = self.land.shape[4]
                 self.publish(m, j, self.land[m, j - 1].reshape(8 * piece, -1).astype(BF))
 
     def end(self):
@@ -354,64 +353,73 @@
     return jnp.concatenate(tiles, axis=1)
 
 
-def attend_block(seq, i, q_ref, k_ref, v_ref, seg_ref, o_ref, lse_ref, bias):
+def attend_block(seq, i, q_ref, k_ref, v_ref, seg_ref, o_ref, lse_ref, bias, between):
     groups = q_ref.shape[1] // GROUP
     back = MAX_DOC // BLK
     here = pl.ds(pl.multiple_of(i * BLK, BLK), BLK)
     row = pl.ds(seq, 1)
     seg_col = column_of(seg_ref[row, here])
-
-    def body(blocks):
-        keys = blocks * BLK
-        start = pl.multiple_of((i + 1 - blocks) * BLK, BLK)
+    count = jnp.minimum(i, back) + 1
+    kinds = range(1, back + 2)
+
+    def first(blocks):
+        return pl.multiple_of((i + 1 - blocks) * BLK, BLK)
+
+    def mask_of(blocks):
+        keys, start = blocks * BLK, first(blocks)
         query = i * BLK + lax.broadcasted_iota(jnp.int32, (BLK, keys), 0)
         key = start + lax.broadcasted_iota(jnp.int32, (BLK, keys), 1)
         allowed = (query >= key) & (seg_col == seg_ref[row, pl.ds(start, keys)])
         bias[:, :keys] = jnp.where(allowed, 0.0, NEG)
 
-        def group(gi, _):
-            parts = []
-            lse = lse_ref[...]
-            head_lane = lax.broadcasted_iota(jnp.int32, (1, LANES), 1)
-            for h in range(HEADS_IN_GROUP):
-                at, off = window_of(h)
-                lanes = pl.ds(pl.multiple_of(gi * GROUP + at, LANES), WIN)
-                mask = lane_mask(off)
-                q = q_ref[here, lanes]
-                q = jnp.where(mask, q, jnp.zeros_like(q))
-                t = nt(q, k_ref[pl.ds(start, keys), lanes]) * (SCALE * LOG2E) + bias[:, :keys]
-                top = jnp.max(t, axis=1, keepdims=True)
-                p = jnp.exp2(t - top)
-                total = jnp.sum(p, axis=1, keepdims=True)
-                o = nn(p.astype(BF), v_ref[pl.ds(start, keys), lanes])
-                parts.append(jnp.where(mask, o * (1.0 / total), 0.0))
-                lse = jnp.where(head_lane == gi * HEADS_IN_GROUP + h, top + jnp.log2(total), lse)
-            lse_ref[...] = lse
-            o_ref[:, pl.ds(pl.multiple_of(gi * GROUP, LANES), GROUP)] = spread(parts).astype(BF)
-            return 0
-
-        lax.fori_loop(0, groups, group, 0)
+    def heads(gi, blocks):
+        keys, start = blocks * BLK, first(blocks)
+        parts = []
+        lse = lse_ref[...]
+        head_lane = lax.broadcasted_iota(jnp.int32, (1, LANES), 1)
+        for h in range(HEADS_IN_GROUP):
+            at, off = window_of(h)
+            lanes = pl.ds(pl.multiple_of(gi * GROUP + at, LANES), WIN)
+            mask = lane_mask(off)
+            q = q_ref[here, lanes]
+            q = jnp.where(mask, q, jnp.zeros_like(q))
+            t = nt(q, k_ref[pl.ds(start, keys), lanes]) * (SCALE * LOG2E) + bias[:, :keys]
+            top = jnp.max(t, axis=1, keepdims=True)
+            p = jnp.exp2(t - top)
+            total = jnp.sum(p, axis=1, keepdims=True)
+            o = nn(p.astype(BF), v_ref[pl.ds(start, keys), lanes])
+            parts.append(jnp.where(mask, o * (1.0 / total), 0.0))
+            lse = jnp.where(head_lane == gi * HEADS_IN_GROUP + h, top + jnp.log2(total), lse)
+        lse_ref[...] = lse
+        o_ref[:, pl.ds(pl.multiple_of(gi * GROUP, LANES), GROUP)] = spread(parts).astype(BF)
 
     lse_ref[...] = jnp.zeros_like(lse_ref)
-    count = jnp.minimum(i, back) + 1
-    for blocks in range(1, back + 2):
-        pl.when(count == blocks)(functools.partial(body, blocks))
+    for blocks in kinds:
+        pl.when(count == blocks)(functools.partial(mask_of, blocks))
+
+    def group(gi, carry):
+        for blocks in kinds:
+            pl.when(count == blocks)(functools.partial(heads, gi, blocks))
+        between(gi)
+        return carry
+
+    lax.fori_loop(0, groups, group, 0)
 
 
 def front_kernel(
-    bits, n, seqs, steps, chunks, count, x_ref, g_ref, c_ref, seg_ref, bias_ref, *refs
+    bits, n, seqs, steps, chunks, count, x_ref, g_ref, c_ref, seg_ref, bq_ref, bv_ref, bh_ref, *refs
 ):
     local, refs = refs[:count], refs[count:]
     n_ref, q_ref, k_ref, v_ref, o_ref, lse_ref, vec_ref, *refs = refs
     full, refs = refs[:count], refs[count:]
-    bias, weights, stage, qs, ks, vs, ns, passing, fresh, land, gather_s, gather_r, mine, raw, bias_in, bias_s, bias_r, local_sem, out_sem, raw_sem, copy_sem, back_sem = refs
+    bias, weights, stage, qs, ks, vs, ns, passing, fresh, land, gather_s, gather_r, mine, raw, bias_in, bias_s, bias_r, local_sem, out_sem, raw_sem, copy_sem, back_sem, bias_ref = refs
     own = local[0].shape[0]
     held_here = weights.shape[0]
     step = pl.program_id(0)
     place = Place(bits)
     shards_ = len(place.on_z)
     ahead = 2 * n + (seqs - 1) * n
-    order = {}
+    order = sorted({chunk[:2] for chunk in chunks if chunk[0] >= held_here}, key=lambda one: max(k for k, chunk in enumerate(chunks) if chunk[:2] == one))
 
     def rows_of(j):
         return pl.ds(j * own, own)
@@ -424,8 +432,7 @@
         if m < held_here:
             weights[m, rows_of(j)] = shard
             return
-        number = len(order)
-        order[number] = m, j
+        number = order.index((m, j))
         if number >= 2:
             stage_copy(number - 2).wait()
         stage[number % 2] = shard
@@ -471,6 +478,12 @@
             if m == 0:
                 for k in range(AHEAD):
                     work.start_z(k)
+        bias_ref[...] = jnp.zeros_like(bias_ref)
+        for r, ref in enumerate((bq_ref, bv_ref, bh_ref)):
+            row = line(ref)
+            for j in range(shards_):
+                pieces = [jnp.zeros((1, j * own), F32), row, jnp.zeros((1, (shards_ - 1 - j) * own), F32)]
+                bias_ref[j, r : r + 1] = jnp.concatenate([t for t in pieces if t.shape[1]], axis=1)
         vectors = [
             send(bias_ref.at[j], bias_in.at[j], (bias_s, bias_r), j, place.on_z[j]) for j in range(1, shards_)
         ]
@@ -585,23 +598,43 @@
             pltpu.make_async_copy(qs.at[there], q_ref.at[there], copy_sem.at[0, b]).wait()
             pltpu.make_async_copy(ks.at[there], k_ref.at[there], copy_sem.at[1, b]).wait()
 
-    @pl.when((step > ahead) & (part >= n))
-    def _():
-        attend_block(seq, part - n, qs, ks, vs, seg_ref, o_ref, lse_ref, bias)
-
     reach = MAX_DOC // BLK + 1
-    attention = [min(i + 1, reach) * ATTEND_COST for i in range(n)]
-    lengths = [1.0] * (ahead + 1) + [1.0] * n + attention + ([1.6] * n + attention) * (seqs - 1)
+    groups = qs.shape[1] // GROUP
+    spots = [(at, None, 1.0) for at in range(1, ahead + 1)]
+    for number in range(seqs):
+        at = 1 + ahead + 2 * n * number
+        spots += [(at + i, None, 1.6 if number else 1.0) for i in range(n)]
+        for i in range(n):
+            each = min(i + 1, reach) * ATTEND_COST / groups
+            spots += [(at + n + i, gi, each) for gi in range(groups)]
     starts = (1, 1 + n, 1 + ahead, steps)
+    where = {}
     for t in range(ready[0], work.ticks):
         m = sum(t >= one for one in ready)
-        first, upto = ready[m - 1], (ready + [work.ticks])[m]
-        span = lengths[starts[m - 1] : starts[m]]
-        goal, at, passed = (t - first + 1) / (upto - first) * sum(span), starts[m - 1], span[0]
-        while passed < goal - 1e-6 and at < starts[m] - 1:
-            at += 1
-            passed += lengths[at]
-        pl.when(step == at)(functools.partial(work.tick, t))
+        begin, upto = ready[m - 1], (ready + [work.ticks])[m]
+        span = [one for one in spots if starts[m - 1] <= one[0] < starts[m]]
+        goal, passed, i = (t - begin + 1) / (upto - begin) * sum(one[2] for one in span), span[0][2], 0
+        while passed < goal - 1e-6 and i < len(span) - 1:
+            i += 1
+            passed += span[i][2]
+        where[t] = span[i][:2]
+
+    def between(gi):
+        for t, (at, spot) in where.items():
+            if spot is not None:
+                pl.when((step == at) & (gi == spot))(functools.partial(work.tick, t))
+
+    for t, (at, spot) in where.items():
+        if spot is None and at <= ahead + n:
+            pl.when(step == at)(functools.partial(work.tick, t))
+
+    @pl.when((step > ahead) & (part >= n))
+    def _():
+        attend_block(seq, part - n, qs, ks, vs, seg_ref, o_ref, lse_ref, bias, between)
+
+    for t, (at, spot) in where.items():
+        if spot is None and at > ahead + n:
+            pl.when(step == at)(functools.partial(work.tick, t))
 
     @pl.when(step == steps - 1)
     def _():
@@ -648,13 +681,13 @@
             whole(g1.shape),
             whole(c1.shape),
             whole(seg.shape),
-            whole(biases.shape),
         ]
+        + [whole((own,))] * 3
         + [anywhere] * count,
-        out_specs=[anywhere] * 4 + [late(out), late(LANES), held(biases.shape[1:])] + [anywhere] * count,
+        out_specs=[anywhere] * 4 + [late(out), late(LANES), held((8, out))] + [anywhere] * count,
         out_shape=[jax.ShapeDtypeStruct((tokens, width), BF)]
         + [jax.ShapeDtypeStruct((tokens, out), BF)] * 4
-        + [jax.ShapeDtypeStruct((tokens, LANES), F32), jax.ShapeDtypeStruct(biases.shape[1:], F32)]
+        + [jax.ShapeDtypeStruct((tokens, LANES), F32), jax.ShapeDtypeStruct((8, out), F32)]
         + [jax.ShapeDtypeStruct((out, width), BF)] * count,
         scratch_shapes=[
             pltpu.VMEM((BLK, BLK + MAX_DOC), F32),
@@ -666,7 +699,7 @@
         + gather_scratch(count, tp, piece, width)
         + [
             pltpu.VMEM((2, 2, piece, width), BF),
-            pltpu.VMEM(biases.shape, F32),
+            pltpu.VMEM((tp, 8, out), F32),
             pltpu.SemaphoreType.DMA((tp,)),
             pltpu.SemaphoreType.DMA((tp,)),
             pltpu.SemaphoreType.DMA((count,)),
@@ -674,6 +707,7 @@
             pltpu.SemaphoreType.DMA((2, 2)),
             pltpu.SemaphoreType.DMA((5, n)),
             pltpu.SemaphoreType.DMA((2,)),
+            pltpu.VMEM((tp, 8, out), F32),
         ],
         compiler_params=hosting(1, 0),
         cost_estimate=pl.CostEstimate(
@@ -682,7 +716,7 @@
             transcendentals=int(pairs),
         ),
         name="front",
-    )(x, g1, c1, seg, biases, *shards_)
+    )(x, g1, c1, seg, *biases, *shards_)
 
 
 def attend_back_kernel(
@@ -946,7 +980,7 @@
 
 def finish_kernel(
     bits, own, steps, dq_ref, dk_ref, dv_ref, x_ref, dr_ref, g_ref, wq_ref, wk_ref, wv_ref, mq_ref, mk_ref, mv_ref, n_ref, in_ref,
-    dx_ref, gq_ref, gk_ref, gv_ref, small_ref, vec, part, acc, taken, *refs,
+    dx_ref, gq_ref, gk_ref, gv_ref, small_ref, vec, part, acc, taken, weights, weight_sem, *refs,
 ):
     step = pl.program_id(0)
     grads = (mq_ref, mk_ref, mv_ref)
@@ -961,8 +995,14 @@
         work = Reduce(place, part, refs[:-3], FINISH_PLAN, publish)
         box, *sems = refs[-3:]
 
+    loads = [
+        pltpu.make_async_copy(src, weights.at[m], weight_sem.at[m]) for m, src in enumerate((wq_ref, wk_ref, wv_ref))
+    ]
+
     @pl.when(step == 0)
     def _():
+        for one in loads:
+            one.start()
         vec[...] = jnp.zeros_like(vec)
         small_ref[...] = in_ref[...]
         if bits is not None:
@@ -995,13 +1035,18 @@
         for m in range(count):
             pl.when(step == m)(functools.partial(work.point, m))
 
+    @pl.when(step == count)
+    def _():
+        for one in loads:
+            one.wait()
+
     @pl.when(step >= count)
     def _():
-        acc[...] = nn(dq_ref[...], wq_ref[...])
+        acc[...] = nn(dq_ref[...], weights[0])
         points(count, count, 3)
-        acc[...] += nn(dk_ref[...], wk_ref[...])
+        acc[...] += nn(dk_ref[...], weights[1])
         points(count + 1, count, 3)
-        d_normed = acc[...] + nn(dv_ref[...], wv_ref[...])
+        d_normed = acc[...] + nn(dv_ref[...], weights[2])
         hat, inv = normalize(x_ref[...].astype(F32))
         d_hat = d_normed * line(g_ref)
         dx_ref[...] = dr_ref[...] + inv * (
@@ -1050,7 +1095,7 @@
         grid=(count + tokens // BLK,),
         in_specs=[late(inner)] * 3
         + [late(width), late(width), whole((width,))]
-        + [whole((inner, width))] * 3
+        + [pl.BlockSpec(memory_space=pl.ANY)] * 3
         + [mine] * 3
         + [whole((tokens, width)), whole((8, width))],
         out_specs=[late(width)] + [held((own, width))] * 3 + [held((8, width))],
@@ -1062,6 +1107,8 @@
             pltpu.VMEM((count, own, width), F32),
             pltpu.VMEM((BLK, width), F32),
             pltpu.VMEM((tokens, pad), BF),
+            pltpu.VMEM((3, inner, width), BF),
+            pltpu.SemaphoreType.DMA((3,)),
         ]
         + (
             reduce_scratch(count, own, width)
@@ -1083,12 +1130,8 @@
     own = wq.shape[1]
     bits = bits_of(dp) if dp == 8 else None
 
-    own_biases = jnp.stack([bq, bv, b1])
-    own_biases = jnp.concatenate([jnp.tile(own_biases, (1, tp)), jnp.zeros((5, tp * own), F32)], axis=0)
-    place = lax.broadcasted_iota(jnp.int32, (tp, 8, tp * own), 2) // own
-    biases = jnp.where(place == lax.broadcasted_iota(jnp.int32, place.shape, 0), own_biases[None], 0.0)
     normed1, q, k, v, mixed, lse, vectors, fq, fk, fv, fo, f1, f2 = front(
-        x, g1, c1, seg, biases, [wq.T, wk.T, wv.T, wo, w1.T, w2], dp, tp
+        x, g1, c1, seg, (bq, bv, b1), [wq.T, wk.T, wv.T, wo, w1.T, w2], dp, tp
     )
 
     y, d_resid, d_mixed, parts, small, rms = middle(

time: 379 us -> 372 us (0.982)
  Pallas kernels: 355 us -> 351 us
    pallas_call x1, Pallas kernels: 68.1 us -> 64.2 us  [finish(): pl.pallas_call(functools.partial(finish_kernel, bits, own, count + tokens...]
where the time goes in v1:
time: 372 us; the launch traced here: 371 us
  Pallas kernels  351 us (94%)
  local copies, waits for them, and re-layouts  19.9 us (5%)
    pallas_call x1, Pallas kernels, front(): pl.pallas_call(functools.partial(front_kernel, bits, n, seqs, steps, chun...  155 us
    pallas_call x1, Pallas kernels, middle(): pl.pallas_call(functools.partial(middle_kernel, own), grid=(n,), in_specs...  69.3 us
    pallas_call x1, Pallas kernels, finish(): pl.pallas_call(functools.partial(finish_kernel, bits, own, count + tokens...  64.2 us
    pallas_call x1, Pallas kernels, attend_back(): pl.pallas_call(functools.partial(attend_back_kernel, seqs * n, bits), gri...  62.2 us
    unnamed x19, local copies, waits for them, and re-layouts  16.7 us

profile of v1, /device:TPU:0, one launch (start us, length us, event | category | flops | bytes accessed | tf_op | source)
XLA Modules:
  0.0 371.4 jit_solution(5931598743591149072)
XLA Ops:
  0.7 155.1 %front.1 = (bf16[2048,1280]{1,0:T(8,128)(2,1)}, bf16[2048,1280]{1,0:T(8,128)(2,1)}, bf16[2048,1280]{1,0:T(8,128)(2,1)}, bf16[2048,1280]{1,0:T(8,128)(2,1)}, bf16...) custom-call(bf16[2048,1280]{1,0:T(8,128)(2,1)} %x_ref.5, ...), custom_call_target="tpu_custom_call" | custom-call | flops 41607495680 | bytes 70778880 | tf_op jit(solution)/shard_map/front/pallas_call | solution.py:676
  155.7 69.3 %middle.1 = (bf16[2048,1280]{1,0:T(8,128)(2,1)}, f32[2048,1280]{1,0:T(8,128)}, bf16[2048,1280]{1,0:T(8,128)(2,1)}, f32[3,320,1280]{2,1,0:T(8,128)}, f32[8,1280]{1,0:T(8,128)}, /*index=5*/f32[2,3]{1,0:T(2,128)}) custom-call(bf16[2048,1280]{1,0:T(8,128)(2,1)} %get-tuple-element.48.m_ref.o_ref, bf16[2048,1280]{1,0:T(8,128)(2,1)} %x_ref.5, ...), custom_call_target="tpu_custom_call" | custom-call | flops 45298483200 | bytes 46530560 | tf_op jit(solution)/shard_map/middle/pallas_call | solution.py:947
  225.1 62.2 %attend_back.1 = (bf16[2048,1280]{1,0:T(8,128)(2,1)}, bf16[2048,1280]{1,0:T(8,128)(2,1)}, bf16[2048,1280]{1,0:T(8,128)(2,1)}, f32[320,1280]{1,0:T(8,128)}, f32[320,1280]{1,0:T(8,128)}, /*index=5*/f32[320,1280]{1,0:T(8,128)}) custom-call(bf16[2048,1280]{1,0:T(8,128)(2,1)} %get-tuple-element.54.q_ref, bf16[2048,1280]{1,0:T(8,128)(2,1)} %get-tuple-element.55.do_ref, ...), custom_call_target="tpu_custom_call" | custom-call | flops 53687091200 | bytes 41943040 | tf_op jit(solution)/shard_map/attend_back/pallas_call | solution.py:829
  287.3 64.2 %finish.1 = (f32[2048,1280]{1,0:T(8,128)}, f32[320,1280]{1,0:T(8,128)}, f32[320,1280]{1,0:T(8,128)}, f32[320,1280]{1,0:T(8,128)}, f32[8,1280]{1,0:T(8,128)}) custom-call(bf16[2048,1280]{1,0:T(8,128)(2,1)} %get-tuple-element.60.dq_ref.mq_ref, bf16[2048,1280]{1,0:T(8,128)(2,1)} %get-tuple-element.61.dk_ref.mk_ref, ...), custom_call_target="tpu_custom_call" | custom-call | flops 20132659200 | bytes 51773440 | tf_op jit(solution)/shard_map/finish/pallas_call | solution.py:1093
  351.4 1.4 slice_reduce_fusion.6
  352.8 1.8 slice_reduce_fusion
  354.6 0.0 copy-start.5
  354.6 8.9 %copy.44 = f32[2048,1280]{1,0:T(8,128)} copy(f32[2048,1280]{1,0:T(8,128)} %get-tuple-element.106) | data formatting | bytes 20971520
  363.5 0.0 copy-done.5
  363.5 0.0 copy-start.4
  363.5 0.0 copy-start.3
  363.5 1.2 copy.45
  364.7 0.9 copy-done.4
  365.5 0.0 copy-start.2
  365.5 1.2 copy.46
  366.7 0.0 copy-done.3
  366.7 0.0 copy-start.1
  366.7 1.2 copy.47
  367.8 0.0 copy-done.2
  367.9 1.2 copy.48
  369.0 0.0 copy-done.1
  369.0 1.2 copy.49
  370.2 0.0 copy-done
  370.2 1.2 copy.50
  (1 shorter events, 0.0 us)
Async XLA Ops:
  354.6 8.9 %copy-start.5 = (f32[320,1280]{1,0:T(8,128)S(1)}, f32[320,1280]{1,0:T(8,128)}, u32[]{:S(2)}) copy-start(f32[320,1280]{1,0:T(8,128)} %get-tuple-element.71) | copy-start | bytes 4915204
  363.5 2.0 copy-start.4
  363.5 3.2 copy-start.3
  365.5 2.3 copy-start.2
  366.7 2.3 copy-start.1
  367.8 2.3 copy-start

commit v2 on v1

--- a/solution.py
+++ b/solution.py
@@ -980,7 +980,7 @@
 
 def finish_kernel(
     bits, own, steps, dq_ref, dk_ref, dv_ref, x_ref, dr_ref, g_ref, wq_ref, wk_ref, wv_ref, mq_ref, mk_ref, mv_ref, n_ref, in_ref,
-    dx_ref, gq_ref, gk_ref, gv_ref, small_ref, vec, part, acc, taken, weights, weight_sem, *refs,
+    dx_ref, gq_ref, gk_ref, gv_ref, small_ref, vec, part, acc, taken, taken_sem, weights, weight_sem, *refs,
 ):
     step = pl.program_id(0)
     grads = (mq_ref, mk_ref, mv_ref)
@@ -1001,22 +1001,30 @@
 
     @pl.when(step == 0)
     def _():
-        for one in loads:
-            one.start()
         vec[...] = jnp.zeros_like(vec)
         small_ref[...] = in_ref[...]
         if bits is not None:
             greet(place.plane())
 
-    def take(m):
-        taken[...] = grads[m][...]
+    def exchange():
+        return [send(small_ref, box.at[place.d], sems, i, peer) for i, peer in enumerate(place.plane())]
+
+    strips = [
+        pltpu.make_async_copy(src.at[:, pl.ds(0, taken.shape[2])], taken.at[m], taken_sem.at[m])
+        for m, src in enumerate(grads)
+    ]
+
+    @pl.when(step == 0)
+    def _():
+        for one in strips + loads:
+            one.start()
 
     for m in range(count):
-        pl.when(step == m)(functools.partial(take, m))
+        pl.when(step == m)(strips[m].wait)
 
     @pl.when(step < count)
     def _():
-        mine = taken[:, :own]
+        mine = taken[step][:, :own]
         part[step] = tn(mine, n_ref[...])
         total = jnp.sum(mine.astype(F32), axis=0, keepdims=True)
         for m in (0, 2):
@@ -1054,23 +1062,27 @@
         )
         vec[0] += fold8(d_normed * hat)
         vec[1] += fold8(d_normed)
+
+        @pl.when(step == steps - 1)
+        def _():
+            for at in range(2):
+                small_ref[4 + at : 5 + at] = jnp.sum(vec[at], axis=0, keepdims=True)
+            if bits is not None:
+                box[place.d] = small_ref[...]
+                for one in exchange():
+                    one.start()
+
         points(count + 2, count, 3)
 
     @pl.when(step == steps - 1)
     def _():
-        for at in range(2):
-            small_ref[4 + at : 5 + at] = jnp.sum(vec[at], axis=0, keepdims=True)
         if bits is None:
             for m in range(count):
                 publish(m, part[m])
         else:
-            copies = [send(small_ref, box.at[place.d], sems, i, peer) for i, peer in enumerate(place.plane())]
-            for one in copies:
-                one.start()
-            box[place.d] = small_ref[...]
-            for one in copies:
+            for one in exchange():
                 one.wait_recv()
-            for one in copies:
+            for one in exchange():
                 one.wait_send()
             total = box[0]
             for i in range(1, 8):
@@ -1085,7 +1097,6 @@
     hosted = bits is not None
     count = 3
     pad = -(-own // LANES) * LANES
-    mine = pl.BlockSpec((tokens, pad), lambda i: (0, 0), pipeline_mode=pl.Buffered(1))
 
     def late(size):
         return pl.BlockSpec((BLK, size), lambda i: (jnp.maximum(i - count, 0), 0))
@@ -1096,7 +1107,7 @@
         in_specs=[late(inner)] * 3
         + [late(width), late(width), whole((width,))]
         + [pl.BlockSpec(memory_space=pl.ANY)] * 3
-        + [mine] * 3
+        + [pl.BlockSpec(memory_space=pl.ANY)] * 3
         + [whole((tokens, width)), whole((8, width))],
         out_specs=[late(width)] + [held((own, width))] * 3 + [held((8, width))],
         out_shape=[jax.ShapeDtypeStruct((tokens, width), F32)]
@@ -1106,7 +1117,8 @@
             pltpu.VMEM((2, 8, width), F32),
             pltpu.VMEM((count, own, width), F32),
             pltpu.VMEM((BLK, width), F32),
-            pltpu.VMEM((tokens, pad), BF),
+            pltpu.VMEM((count, tokens, pad), BF),
+            pltpu.SemaphoreType.DMA((count,)),
             pltpu.VMEM((3, inner, width), BF),
             pltpu.SemaphoreType.DMA((3,)),
         ]

time: 372 us -> 370 us (level)
  no operation moved by 1% of the time
where the time goes in v2:
time: 370 us; the launch traced here: 369 us
  Pallas kernels  349 us (94%)
  local copies, waits for them, and re-layouts  19.9 us (5%)
    pallas_call x1, Pallas kernels, front(): pl.pallas_call(functools.partial(front_kernel, bits, n, seqs, steps, chun...  155 us
    pallas_call x1, Pallas kernels, middle(): pl.pallas_call(functools.partial(middle_kernel, own), grid=(n,), in_specs...  69.3 us
    pallas_call x1, Pallas kernels, finish(): pl.pallas_call(functools.partial(finish_kernel, bits, own, count + tokens...  62.3 us
    pallas_call x1, Pallas kernels, attend_back(): pl.pallas_call(functools.partial(attend_back_kernel, seqs * n, bits), gri...  62.2 us
    unnamed x19, local copies, waits for them, and re-layouts  16.7 us

profile of v2, /device:TPU:0, one launch (start us, length us, event | category | flops | bytes accessed | tf_op | source)
XLA Modules:
  0.0 369.5 jit_solution(6296440756530291539)
XLA Ops:
  0.7 155.1 %front.1 = (bf16[2048,1280]{1,0:T(8,128)(2,1)}, bf16[2048,1280]{1,0:T(8,128)(2,1)}, bf16[2048,1280]{1,0:T(8,128)(2,1)}, bf16[2048,1280]{1,0:T(8,128)(2,1)}, bf16...) custom-call(bf16[2048,1280]{1,0:T(8,128)(2,1)} %x_ref.5, ...), custom_call_target="tpu_custom_call" | custom-call | flops 41607495680 | bytes 70778880 | tf_op jit(solution)/shard_map/front/pallas_call | solution.py:676
  155.7 69.3 %middle.1 = (bf16[2048,1280]{1,0:T(8,128)(2,1)}, f32[2048,1280]{1,0:T(8,128)}, bf16[2048,1280]{1,0:T(8,128)(2,1)}, f32[3,320,1280]{2,1,0:T(8,128)}, f32[8,1280]{1,0:T(8,128)}, /*index=5*/f32[2,3]{1,0:T(2,128)}) custom-call(bf16[2048,1280]{1,0:T(8,128)(2,1)} %get-tuple-element.48.m_ref.o_ref, bf16[2048,1280]{1,0:T(8,128)(2,1)} %x_ref.5, ...), custom_call_target="tpu_custom_call" | custom-call | flops 45298483200 | bytes 46530560 | tf_op jit(solution)/shard_map/middle/pallas_call | solution.py:947
  225.1 62.2 %attend_back.1 = (bf16[2048,1280]{1,0:T(8,128)(2,1)}, bf16[2048,1280]{1,0:T(8,128)(2,1)}, bf16[2048,1280]{1,0:T(8,128)(2,1)}, f32[320,1280]{1,0:T(8,128)}, f32[320,1280]{1,0:T(8,128)}, /*index=5*/f32[320,1280]{1,0:T(8,128)}) custom-call(bf16[2048,1280]{1,0:T(8,128)(2,1)} %get-tuple-element.54.q_ref, bf16[2048,1280]{1,0:T(8,128)(2,1)} %get-tuple-element.55.do_ref, ...), custom_call_target="tpu_custom_call" | custom-call | flops 53687091200 | bytes 41943040 | tf_op jit(solution)/shard_map/attend_back/pallas_call | solution.py:829
  287.3 62.3 %finish.1 = (f32[2048,1280]{1,0:T(8,128)}, f32[320,1280]{1,0:T(8,128)}, f32[320,1280]{1,0:T(8,128)}, f32[320,1280]{1,0:T(8,128)}, f32[8,1280]{1,0:T(8,128)}) custom-call(bf16[2048,1280]{1,0:T(8,128)(2,1)} %get-tuple-element.60.dq_ref.mq_ref, bf16[2048,1280]{1,0:T(8,128)(2,1)} %get-tuple-element.61.dk_ref.mk_ref, ...), custom_call_target="tpu_custom_call" | custom-call | flops 20132659200 | bytes 51773440 | tf_op jit(solution)/shard_map/finish/pallas_call | solution.py:1104
  349.6 1.4 slice_reduce_fusion.6
  351.0 1.8 slice_reduce_fusion
  352.8 0.0 copy-start.5
  352.8 8.9 %copy.44 = f32[2048,1280]{1,0:T(8,128)} copy(f32[2048,1280]{1,0:T(8,128)} %get-tuple-element.106) | data formatting | bytes 20971520
  361.6 0.0 copy-done.5
  361.6 0.0 copy-start.4
  361.6 0.0 copy-start.3
  361.6 1.2 copy.45
  362.8 0.9 copy-done.4
  363.7 0.0 copy-start.2
  363.7 1.2 copy.46
  364.8 0.0 copy-done.3
  364.8 0.0 copy-start.1
  364.8 1.2 copy.47
  366.0 0.0 copy-done.2
  366.0 1.2 copy.48
  367.2 0.0 copy-done.1
  367.2 1.2 copy.49
  368.3 0.0 copy-done
  368.3 1.2 copy.50
  (1 shorter events, 0.0 us)
Async XLA Ops:
  352.8 8.9 %copy-start.5 = (f32[320,1280]{1,0:T(8,128)S(1)}, f32[320,1280]{1,0:T(8,128)}, u32[]{:S(2)}) copy-start(f32[320,1280]{1,0:T(8,128)} %get-tuple-element.71) | copy-start | bytes 4915204
  361.6 2.0 copy-start.4
  361.6 3.2 copy-start.3
  363.7 2.3 copy-start.2
  364.8 2.3 copy-start.1
  366.0 2.3 copy-start
